TPU v7x, 32 devices: a whole 2x2x4 slice. The times are simulated.
32 devices in a mesh: dp: 4 (over z), ctx: 2 (over x), hidden: 4 (over y, core).
Axes of the slice: x: 2, y: 2, z: 4, core: 2. Of those that a mesh axis runs over, the one named last changes fastest.
Arguments:
- activations: bfloat16 [4, 1024, 53248], P('dp', 'ctx', 'hidden'), may hold values from -6 to 6
- out_grads: bfloat16 [4, 1024, 16384], P('dp', 'ctx', 'hidden'), may hold values from -0.1875 to 0.1875
- input_basis: bfloat16 [53248, 512], P('hidden', ('dp', 'ctx')), may hold values from -0.02734375 to 0.02734375
- output_basis: bfloat16 [16384, 512], P('hidden', ('dp', 'ctx')), may hold values from -0.046875 to 0.046875
- rotation: bfloat16 [512, 512], P('ctx'), may hold values from -0.25 to 0.25
Outputs:
- logged: float32 [4, 512, 512], P('dp', 'ctx', 'hidden')
All inputs are finite; a program needn't handle non-finite values.
Results may differ from a plain program's by a relative error of at most 0.0049.
Values may be sent and summed in bfloat16 or wider, within the bound.
A program may use at most 64 MiB of HBM per device.

v0:
```python
import jax
import jax.numpy as jnp
from jax import lax
from jax.sharding import PartitionSpec as P


def outer_sum(left, right):
    return lax.dot_general(
        left, right, (((0,), (0,)), ((), ())), preferred_element_type=jnp.float32
    )


def local(activations, out_grads, input_basis, output_basis, rotation):
    tokens = activations.reshape(-1, activations.shape[-1])
    grad_rows = out_grads.reshape(-1, out_grads.shape[-1])
    in_part = jnp.dot(
        tokens,
        lax.all_gather(input_basis, ("dp", "ctx"), axis=1, tiled=True),
        preferred_element_type=jnp.float32,
    )
    out_part = jnp.dot(
        grad_rows,
        lax.all_gather(output_basis, ("dp", "ctx"), axis=1, tiled=True),
        preferred_element_type=jnp.float32,
    )
    in_cols = lax.psum_scatter(in_part, "hidden", scatter_dimension=1, tiled=True).astype(
        jnp.bfloat16
    )
    out_side = lax.psum(out_part, "hidden")
    out_side = out_side.astype(jnp.bfloat16)
    total = lax.psum(outer_sum(out_side, in_cols), "ctx")
    lowrank = total.astype(jnp.bfloat16)
    logged = jnp.dot(rotation, lowrank, preferred_element_type=jnp.float32)
    return logged.reshape(1, logged.shape[0], logged.shape[1])


def solution(mesh):
    return jax.shard_map(
        local,
        mesh=mesh,
        in_specs=(
            P("dp", "ctx", "hidden"),
            P("dp", "ctx", "hidden"),
            P("hidden", ("dp", "ctx")),
            P("hidden", ("dp", "ctx")),
            P("ctx", None),
        ),
        out_specs=P("dp", "ctx", "hidden"),
        check_vma=False,
    )
```

profile of v0, /device:TPU:0, one launch (start us, length us, event | category | flops | bytes accessed | tf_op | source)
XLA Modules:
  0.0 329.6 jit_solution(16970726115371257310)
XLA Ops:
  6.5 0.0 copy-start
  6.5 0.0 all-gather.5.cloned.1.call-start
  6.5 0.7 all-gather.5.cloned.1.call-update
  7.3 0.0 all-gather.3.cloned.1.call-start
  7.3 0.7 all-gather.3.cloned.1.call-update
  8.0 0.0 reduce-scatter.2.cloned.1.call-start
  8.1 193.1 %all-gather.5.cloned.1.call-done = bf16[13312,512]{0,1:T(8,128)(2,1)} async-done(((bf16[13312,64]{0,1:T(8,128)(2,1)}), bf16[13312,512]{0,1:T(8,128)(2,1)}) %all-gather.5.cloned.1.call-update) | async-done | bytes 13631504 | tf_op jit(solution)/shard_map/all_gather | solution.py:18
  201.2 15.1 %fusion = f32[512,512]{1,0:T(8,128)} fusion(bf16[13312,512]{0,1:T(8,128)(2,1)} %all-gather.5.cloned.1.call-done, bf16[1,512,13312]{2,1,0:T(8,128)(2,1)} %param.5), kind=kOutput, calls=%fused_computation | convolution fusion | flops 6979321856 | bytes 28311552 | tf_op jit(solution)/shard_map/dot_general | solution.py:16
  216.3 0.0 reduce-scatter.2.cloned.1.call-update
  216.3 58.0 %all-gather.3.cloned.1.call-done = bf16[4096,512]{0,1:T(8,128)(2,1)} async-done(((bf16[4096,64]{0,1:T(8,128)(2,1)}), bf16[4096,512]{0,1:T(8,128)(2,1)}) %all-gather.3.cloned.1.call-update) | async-done | bytes 4194320 | tf_op jit(solution)/shard_map/all_gather | solution.py:23
  274.3 5.8 %fusion.2 = f32[512,512]{1,0:T(8,128)S(1)} fusion(bf16[4096,512]{0,1:T(8,128)(2,1)} %all-gather.3.cloned.1.call-done, bf16[1,512,4096]{2,1,0:T(8,128)(2,1)} %param.6), kind=kOutput, calls=%fused_computation.2 | convolution fusion | flops 2147483648 | bytes 9437184 | tf_op jit(solution)/shard_map/dot_general | solution.py:21
  280.1 28.4 %all-reduce.2 = bf16[512,512]{1,0:T(8,128)(2,1)S(1)} all-reduce(f32[512,512]{1,0:T(8,128)S(1)} %fusion.2), channel_id=1, replica_groups=mesh['dp'=4,'ctx'=2,'hidden'=4] {'hidden'}, use_global_device_ids=true, to_apply=%region_0.0 | all-reduce | flops 262144 | bytes 1572864 | tf_op jit(solution)/shard_map/psum | solution.py:29
  308.5 0.0 reduce-scatter.2.cloned.1.call-done
  308.6 1.3 fusion.4
  309.8 12.2 %all-reduce.3 = bf16[512,128]{1,0:T(8,128)(2,1)S(1)} all-reduce(f32[512,128]{1,0:T(8,128)S(1)} %fusion.4), channel_id=1, replica_groups=mesh['dp'=4,'ctx'=2,'hidden'=4] {'ctx'}, use_global_device_ids=true, to_apply=%region_2.0 | all-reduce | flops 65536 | bytes 393216 | tf_op jit(solution)/shard_map/psum | solution.py:31
  322.1 0.0 copy-done
  322.1 0.2 convolution_bitcast_fusion
  322.3 0.8 copy.6
Async XLA Ops:
  6.5 315.5 %copy-start = (bf16[256,512]{1,0:T(8,128)(2,1)S(1)}, bf16[256,512]{1,0:T(8,128)(2,1)}, u32[]{:S(2)}) copy-start(bf16[256,512]{1,0:T(8,128)(2,1)} %param.9) | copy-start | bytes 786436
  6.5 194.6 %all-gather.5.cloned.1.call-start = ((), (), s32[]{:S(2)}) async-start(), calls=%async_computation.2 | async-start | bytes 15335424 | tf_op jit(solution)/shard_map/all_gather | solution.py:18
  7.3 267.0 %all-gather.3.cloned.1.call-start = ((), (), s32[]{:S(2)}) async-start(), calls=%async_computation.1 | async-start | bytes 4718592 | tf_op jit(solution)/shard_map/all_gather | solution.py:23
  8.0 300.5 %reduce-scatter.2.cloned.1.call-start = ((), (), s32[]{:S(2)}) async-start(), calls=%async_computation.3 | async-start | bytes 1310720 | tf_op jit(solution)/shard_map/reduce_scatter | solution.py:26
Sparse Core Ops, SparseCore 0:
  9.5 191.5 all-gather.4
  203.3 70.9 all-gather.2
  276.8 26.8 reduce-scatter.1
where the time goes:
time: 330 us
  waiting for transfers between devices  253 us (77%)
  blocking collectives  40.6 us (12%)
  matrix products  22.5 us (7%)
  between operations  13.2 us (4%)
    all_gather x1, waiting for transfers between devices, local(): lax.all_gather(input_basis, ('dp', 'ctx'), axis=1, tiled=True)  193 us
    all_gather x1, waiting for transfers between devices, local(): lax.all_gather(output_basis, ('dp', 'ctx'), axis=1, tiled=True)  58 us
    psum x1, blocking collectives, local(): out_side = lax.psum(out_part, 'hidden')  28.4 us
    dot_general x1, matrix products, local(): jnp.dot(tokens, lax.all_gather(input_basis, ('dp', 'ctx'), axis=1, tiled=...  15.1 us
    psum x1, blocking collectives, local(): total = lax.psum(outer_sum(out_side, in_cols), 'ctx')  12.2 us
  transfers between devices with their start and end apart: 3, of which 2 were waited for; matrix products, arithmetic and copies ran while one was open for 6% of the time, Pallas kernels for 0%

commit v1 on v0

--- a/solution.py
+++ b/solution.py
@@ -1,7 +1,15 @@
+import functools
 import jax
 import jax.numpy as jnp
 from jax import lax
 from jax.sharding import PartitionSpec as P
+
+
+def part_chunk(panel, which_axis):
+    return jnp.sum(lax.all_gather(panel, which_axis), 0)
+
+
+_drive_notes = functools.partial(part_chunk, which_axis="hidden")
 
 
 def outer_sum(left, right):
@@ -26,7 +34,7 @@
     in_cols = lax.psum_scatter(in_part, "hidden", scatter_dimension=1, tiled=True).astype(
         jnp.bfloat16
     )
-    out_side = lax.psum(out_part, "hidden")
+    out_side = _drive_notes(out_part)
     out_side = out_side.astype(jnp.bfloat16)
     total = lax.psum(outer_sum(out_side, in_cols), "ctx")
     lowrank = total.astype(jnp.bfloat16)

time: 330 us -> 356 us (1.079)
  waiting for transfers between devices: 253 us -> 304 us
  blocking collectives: 40.6 us -> 11.3 us
    psum x1 -> x0, blocking collectives: 28.4 us -> none  [local(): out_side = lax.psum(out_part, 'hidden')]
    reduce_scatter x1, waiting for transfers between devices: 0.02 us -> 24.5 us  [local(): lax.psum_scatter(in_part, 'hidden', scatter_dimension=1, tiled=True)]
    all_gather x1, waiting for transfers between devices: 58 us -> 76.9 us  [local(): lax.all_gather(output_basis, ('dp', 'ctx'), axis=1, tiled=True)]
    all_gather x0 -> x1, waiting for transfers between devices: none -> 18.7 us  [part_chunk(): return jnp.sum(lax.all_gather(panel, which_axis), 0)]
    all_gather x1, waiting for transfers between devices: 193 us -> 183 us  [local(): lax.all_gather(input_basis, ('dp', 'ctx'), axis=1, tiled=True)]
  transfers between devices with their start and end apart: 3 -> 4, of which waited for: 2 -> 4; matrix products, arithmetic and copies ran while one was open for 6% -> 7% of each run, Pallas kernels for 0% -> 0%
where the time goes in v1:
time: 356 us
  waiting for transfers between devices  304 us (85%)
  matrix products  23.9 us (7%)
  between operations  13.2 us (4%)
  blocking collectives  11.3 us (3%)
    all_gather x1, waiting for transfers between devices, local(): lax.all_gather(input_basis, ('dp', 'ctx'), axis=1, tiled=True)  183 us
    all_gather x1, waiting for transfers between devices, local(): lax.all_gather(output_basis, ('dp', 'ctx'), axis=1, tiled=True)  76.9 us
    reduce_scatter x1, waiting for transfers between devices, local(): lax.psum_scatter(in_part, 'hidden', scatter_dimension=1, tiled=True)  24.5 us
    all_gather x1, waiting for transfers between devices, part_chunk(): return jnp.sum(lax.all_gather(panel, which_axis), 0)  18.7 us
    dot_general x1, matrix products, local(): jnp.dot(tokens, lax.all_gather(input_basis, ('dp', 'ctx'), axis=1, tiled=...  15.5 us
    psum x1, blocking collectives, local(): total = lax.psum(outer_sum(out_side, in_cols), 'ctx')  11.3 us
  transfers between devices with their start and end apart: 4, of which 4 were waited for; matrix products, arithmetic and copies ran while one was open for 7% of the time, Pallas kernels for 0%

profile of v1, /device:TPU:0, one launch (start us, length us, event | category | flops | bytes accessed | tf_op | source)
XLA Modules:
  0.0 356.3 jit_solution(15177708152345942377)
XLA Ops:
  6.5 0.0 copy-start
  6.5 0.0 all-gather.5.cloned.1.call-start
  6.5 0.7 all-gather.5.cloned.1.call-update
  7.3 0.0 all-gather.7.cloned.1.call-start
  7.3 0.7 all-gather.7.cloned.1.call-update
  8.0 0.0 all-gather.9.cloned.1.call-start
  8.1 76.9 %all-gather.5.cloned.1.call-done = bf16[4096,512]{0,1:T(8,128)(2,1)} async-done(((bf16[4096,64]{0,1:T(8,128)(2,1)}), bf16[4096,512]{0,1:T(8,128)(2,1)}) %all-gather.5.cloned.1.call-update) | async-done | bytes 4194320 | tf_op jit(solution)/shard_map/all_gather | solution.py:31
  85.0 6.8 %fusion.2 = f32[512,512]{1,0:T(8,128)} fusion(bf16[4096,512]{0,1:T(8,128)(2,1)} %all-gather.5.cloned.1.call-done, bf16[1,512,4096]{2,1,0:T(8,128)(2,1)} %param.6), kind=kOutput, calls=%fused_computation.2 | convolution fusion | flops 2147483648 | bytes 9437184 | tf_op jit(solution)/shard_map/dot_general | solution.py:29
  91.8 0.0 all-gather.9.cloned.1.call-update
  91.9 0.0 reduce-scatter.2.cloned.1.call-start
  91.9 182.7 %all-gather.7.cloned.1.call-done = bf16[13312,512]{0,1:T(8,128)(2,1)} async-done(((bf16[13312,64]{0,1:T(8,128)(2,1)}), bf16[13312,512]{0,1:T(8,128)(2,1)}) %all-gather.7.cloned.1.call-update) | async-done | bytes 13631504 | tf_op jit(solution)/shard_map/all_gather | solution.py:26
  274.6 15.5 %fusion = f32[512,512]{1,0:T(8,128)} fusion(bf16[13312,512]{0,1:T(8,128)(2,1)} %all-gather.7.cloned.1.call-done, bf16[1,512,13312]{2,1,0:T(8,128)(2,1)} %param.5), kind=kOutput, calls=%fused_computation | convolution fusion | flops 6979321856 | bytes 28311552 | tf_op jit(solution)/shard_map/dot_general | solution.py:24
  290.2 0.0 reduce-scatter.2.cloned.1.call-update
  290.2 18.7 %all-gather.9.cloned.1.call-done = f32[2048,512]{1,0:T(8,128)} async-done(((f32[512,512]{1,0:T(8,128)}), f32[2048,512]{1,0:T(8,128)}) %all-gather.9.cloned.1.call-update) | async-done | bytes 4194320 | tf_op jit(solution)/shard_map/all_gather | solution.py:9
  308.9 2.7 reduce_sum.9
  311.6 24.5 %reduce-scatter.2.cloned.1.call-done = f32[512,128]{1,0:T(8,128)} async-done(((f32[512,512]{1,0:T(8,128)}), f32[512,128]{1,0:T(8,128)}) %reduce-scatter.2.cloned.1.call-update) | async-done | bytes 262160 | tf_op jit(solution)/shard_map/reduce_scatter | solution.py:34
  336.1 1.3 fusion.4
  337.4 11.3 %all-reduce.1 = bf16[512,128]{1,0:T(8,128)(2,1)S(1)} all-reduce(f32[512,128]{1,0:T(8,128)S(1)} %fusion.4), channel_id=1, replica_groups=mesh['dp'=4,'ctx'=2,'hidden'=4] {'ctx'}, use_global_device_ids=true, to_apply=%region_2.0 | all-reduce | flops 65536 | bytes 393216 | tf_op jit(solution)/shard_map/psum | solution.py:39
  348.7 0.0 copy-done
  348.8 0.2 convolution_bitcast_fusion
  349.0 0.8 copy.6
Async XLA Ops:
  6.5 342.2 %copy-start = (bf16[256,512]{1,0:T(8,128)(2,1)S(1)}, bf16[256,512]{1,0:T(8,128)(2,1)}, u32[]{:S(2)}) copy-start(bf16[256,512]{1,0:T(8,128)(2,1)} %param.9) | copy-start | bytes 786436
  6.5 78.5 %all-gather.5.cloned.1.call-start = ((), (), s32[]{:S(2)}) async-start(), calls=%async_computation.1 | async-start | bytes 4718592 | tf_op jit(solution)/shard_map/all_gather | solution.py:31
  7.3 267.4 %all-gather.7.cloned.1.call-start = ((), (), s32[]{:S(2)}) async-start(), calls=%async_computation.2 | async-start | bytes 15335424 | tf_op jit(solution)/shard_map/all_gather | solution.py:26
  8.0 300.9 %all-gather.9.cloned.1.call-start = ((), (), s32[]{:S(2)}) async-start(), calls=%async_computation.4 | async-start | bytes 5242880 | tf_op jit(solution)/shard_map/all_gather | solution.py:9
  91.9 244.3 %reduce-scatter.2.cloned.1.call-start = ((), (), s32[]{:S(2)}) async-start(), calls=%async_computation.3 | async-start | bytes 1310720 | tf_op jit(solution)/shard_map/reduce_scatter | solution.py:34
Sparse Core Ops, SparseCore 0:
  9.5 75.4 all-gather.4
  87.2 187.4 all-gather.6
  276.2 32.6 all-gather.8
  311.3 24.8 reduce-scatter.1

commit v2 on v0

--- a/solution.py
+++ b/solution.py
@@ -2,6 +2,18 @@
 import jax.numpy as jnp
 from jax import lax
 from jax.sharding import PartitionSpec as P
+
+
+def doubled_up(x, axis, dim):
+    ways, here, step = (lax.axis_size(axis), lax.axis_index(axis), x.shape[dim])
+    line, have = (x, 1)
+    while have < ways:
+        line = jnp.concatenate(
+            [line, lax.ppermute(line, axis, [(d, (d - have) % ways) for d in range(ways)])],
+            axis=dim,
+        )
+        have = 2 * have
+    return jnp.roll(line, here * step, axis=dim)
 
 
 def outer_sum(left, right):
@@ -19,9 +31,7 @@
         preferred_element_type=jnp.float32,
     )
     out_part = jnp.dot(
-        grad_rows,
-        lax.all_gather(output_basis, ("dp", "ctx"), axis=1, tiled=True),
-        preferred_element_type=jnp.float32,
+        grad_rows, doubled_up(output_basis, ("dp", "ctx"), 1), preferred_element_type=jnp.float32
     )
     in_cols = lax.psum_scatter(in_part, "hidden", scatter_dimension=1, tiled=True).astype(
         jnp.bfloat16

time: 330 us -> 378 us (1.15)
  waiting for transfers between devices: 253 us -> 278 us
  local copies, waits for them, and re-layouts: 0.76 us -> 11.5 us
  starting transfers between devices: 0.08 us -> 6.16 us
  other arithmetic: 0 us -> 3.89 us
    ppermute x0 -> x3, waiting for transfers between devices: none -> 256 us  [doubled_up(): lax.ppermute(line, axis, [(d, (d - have) % ways) for d in range(ways)])]
    all_gather x1, waiting for transfers between devices: 193 us -> 20.9 us  [local(): lax.all_gather(input_basis, ('dp', 'ctx'), axis=1, tiled=True)]
    all_gather x1 -> x0, waiting for transfers between devices: 58 us -> none  [local(): lax.all_gather(output_basis, ('dp', 'ctx'), axis=1, tiled=True)]
    unnamed x2 -> x15, local copies, waits for them, and re-layouts: 0.01 us -> 9.13 us
    ppermute x0 -> x3, starting transfers between devices: none -> 6.12 us  [doubled_up(): lax.ppermute(line, axis, [(d, (d - have) % ways) for d in range(ways)])]
    concatenate x0 -> x2, other arithmetic: none -> 3.89 us  [doubled_up(): jnp.concatenate([line, lax.ppermute(line, axis, [(d, (d - have) % ways) f...]
  transfers between devices with their start and end apart: 3 -> 5, of which waited for: 2 -> 4; matrix products, arithmetic and copies ran while one was open for 6% -> 5% of each run, Pallas kernels for 0% -> 0%
where the time goes in v2:
time: 378 us
  waiting for transfers between devices  278 us (74%)
  blocking collectives  42.3 us (11%)
  matrix products  22.4 us (6%)
  between operations  13.5 us (4%)
  local copies, waits for them, and re-layouts  11.5 us (3%)
  starting transfers between devices  6.16 us (2%)
  other arithmetic  3.89 us (1%)
    ppermute x3, waiting for transfers between devices, doubled_up(): lax.ppermute(line, axis, [(d, (d - have) % ways) for d in range(ways)])  256 us
    psum x1, blocking collectives, local(): out_side = lax.psum(out_part, 'hidden')  29.9 us
    all_gather x1, waiting for transfers between devices, local(): lax.all_gather(input_basis, ('dp', 'ctx'), axis=1, tiled=True)  20.9 us
    dot_general x1, matrix products, local(): jnp.dot(tokens, lax.all_gather(input_basis, ('dp', 'ctx'), axis=1, tiled=...  15.1 us
    psum x1, blocking collectives, local(): total = lax.psum(outer_sum(out_side, in_cols), 'ctx')  12.4 us
    unnamed x15, local copies, waits for them, and re-layouts  9.13 us
  transfers between devices with their start and end apart: 5, of which 4 were waited for; matrix products, arithmetic and copies ran while one was open for 5% of the time, Pallas kernels for 0%

profile of v2, /device:TPU:0, one launch (start us, length us, event | category | flops | bytes accessed | tf_op | source)
XLA Modules:
  0.0 377.7 jit_solution(6404543079348818538)
XLA Ops:
  6.5 0.0 copy-start
  6.5 0.0 all-gather.2.cloned.1.call-start
  6.5 0.7 all-gather.2.cloned.1.call-update
  7.3 0.0 reduce-scatter.2.cloned.1.call-start
  7.3 6.1 %collective-permute-start = (bf16[4096,64]{0,1:T(8,128)(2,1)}, bf16[4096,64]{0,1:T(8,128)(2,1)S(1)}, u32[]{:S(2)}, u32[]{:S(2)}) collective-permute-start(bf16[4096,64]{0,1:T(8,128)(2,1)} %param.8), channel_id=1, source_target_pairs={{0,28},{4,0},{8,4},{12,8},{16,12},{20,16},{24,20},{28,24},{1,29},{... | collective-permute-start | bytes 1572872 | tf_op jit(solution)/shard_map/ppermute | solution.py:12
  13.4 15.4 %collective-permute-done = bf16[4096,64]{0,1:T(8,128)(2,1)S(1)} collective-permute-done((bf16[4096,64]{0,1:T(8,128)(2,1)}, bf16[4096,64]{0,1:T(8,128)(2,1)S(1)}, u32[]{:S(2)}, u32[]{:S(2)}) %collective-permute-start) | collective-permute-done | bytes 524320 | tf_op jit(solution)/shard_map/ppermute | solution.py:12
  28.8 0.0 copy-start.2
  28.8 1.3 pad_maximum_fusion.1
  30.1 0.1 collective-permute-start.1
  30.2 70.2 %collective-permute-done.1 = bf16[4096,128]{0,1:T(8,128)(2,1)S(1)} collective-permute-done((bf16[4096,128]{0,1:T(8,128)(2,1)S(1)}, bf16[4096,128]{0,1:T(8,128)(2,1)S(1)}, u32[]{:S(2)}, u32[]{:S(2)}) %collective-permute-start.1) | collective-permute-done | bytes 1048608 | tf_op jit(solution)/shard_map/ppermute | solution.py:12
  100.3 0.0 copy-done.2
  100.3 2.6 pad_maximum_fusion
  102.9 0.0 collective-permute-start.2
  102.9 0.0 copy-start.1
  102.9 0.0 copy-start.3
  102.9 1.9 constant_dynamic-update-slice_fusion.7
  104.8 1.9 constant_dynamic-update-slice_fusion.6
  106.7 1.1 constant_dynamic-update-slice_fusion.5
  107.8 170.8 %collective-permute-done.2 = bf16[4096,256]{0,1:T(8,128)(2,1)S(1)} collective-permute-done((bf16[4096,256]{0,1:T(8,128)(2,1)}, bf16[4096,256]{0,1:T(8,128)(2,1)S(1)}, u32[]{:S(2)}, u32[]{:S(2)}) %collective-permute-start.2) | collective-permute-done | bytes 2097184 | tf_op jit(solution)/shard_map/ppermute | solution.py:12
  278.6 1.5 constant_dynamic-update-slice_fusion.4
  280.1 0.0 copy-done.1
  280.1 0.8 constant_dynamic-update-slice_fusion.3
  281.0 0.0 copy-done.3
  281.0 0.8 constant_dynamic-update-slice_fusion.2
  281.8 1.1 constant_dynamic-update-slice_fusion.1
  282.9 20.9 %all-gather.2.cloned.1.call-done = bf16[13312,512]{0,1:T(8,128)(2,1)} async-done(((bf16[13312,64]{0,1:T(8,128)(2,1)}), bf16[13312,512]{0,1:T(8,128)(2,1)}) %all-gather.2.cloned.1.call-update) | async-done | bytes 13631504 | tf_op jit(solution)/shard_map/all_gather | solution.py:30
  303.8 15.1 %fusion = f32[512,512]{1,0:T(8,128)} fusion(bf16[13312,512]{0,1:T(8,128)(2,1)} %all-gather.2.cloned.1.call-done, bf16[1,512,13312]{2,1,0:T(8,128)(2,1)} %param.5), kind=kOutput, calls=%fused_computation | convolution fusion | flops 6979321856 | bytes 28311552 | tf_op jit(solution)/shard_map/dot_general | solution.py:28
  318.9 0.0 reduce-scatter.2.cloned.1.call-update
  318.9 1.6 constant_dynamic-update-slice_fusion
  320.5 5.8 %fusion.5 = f32[512,512]{0,1:T(8,128)S(1)} fusion(bf16[1,512,4096]{2,1,0:T(8,128)(2,1)} %param.6, bf16[4096,1024]{0,1:T(8,128)(2,1)} %constant_dynamic-update-slice_fusion, s32[]{:T(128)S(6)} %select_n.14), kind=kOutput, calls=%fused_computation.6 | convolution fusion | flops 2147483648 | bytes 9437188 | tf_op jit(solution)/shard_map/dot_general | solution.py:33
  326.3 29.9 %all-reduce.2 = bf16[512,512]{0,1:T(8,128)(2,1)S(1)} all-reduce(f32[512,512]{0,1:T(8,128)S(1)} %fusion.5), channel_id=1, replica_groups=mesh['dp'=4,'ctx'=2,'hidden'=4] {'hidden'}, use_global_device_ids=true, to_apply=%region_0.1 | all-reduce | flops 262144 | bytes 1572864 | tf_op jit(solution)/shard_map/psum | solution.py:39
  356.2 0.0 reduce-scatter.2.cloned.1.call-done
  356.2 1.2 fusion.10
  357.5 12.4 %all-reduce.3 = bf16[512,128]{1,0:T(8,128)(2,1)S(1)} all-reduce(f32[512,128]{1,0:T(8,128)S(1)} %fusion.10), channel_id=1, replica_groups=mesh['dp'=4,'ctx'=2,'hidden'=4] {'ctx'}, use_global_device_ids=true, to_apply=%region_2.3 | all-reduce | flops 65536 | bytes 393216 | tf_op jit(solution)/shard_map/psum | solution.py:41
  369.8 0.0 copy-done
  369.8 0.2 convolution_bitcast_fusion
  370.1 0.8 copy.6
Async XLA Ops:
  6.5 363.3 %copy-start = (bf16[256,512]{1,0:T(8,128)(2,1)S(1)}, bf16[256,512]{1,0:T(8,128)(2,1)}, u32[]{:S(2)}) copy-start(bf16[256,512]{1,0:T(8,128)(2,1)} %param.9) | copy-start | bytes 786436
  6.5 297.2 %all-gather.2.cloned.1.call-start = ((), (), s32[]{:S(2)}) async-start(), calls=%async_computation.1 | async-start | bytes 15335424 | tf_op jit(solution)/shard_map/all_gather | solution.py:30
  7.3 349.0 %reduce-scatter.2.cloned.1.call-start = ((), (), s32[]{:S(2)}) async-start(), calls=%async_computation.2 | async-start | bytes 1310720 | tf_op jit(solution)/shard_map/reduce_scatter | solution.py:36
  7.3 21.5 %collective-permute-start = (bf16[4096,64]{0,1:T(8,128)(2,1)}, bf16[4096,64]{0,1:T(8,128)(2,1)S(1)}, u32[]{:S(2)}, u32[]{:S(2)}) collective-permute-start(bf16[4096,64]{0,1:T(8,128)(2,1)} %param.8), channel_id=1, source_target_pairs={{0,28},{4,0},{8,4},{12,8},{16,12},{20,16},{24,20},{28,24},{1,29},{... | collective-permute-start | bytes 1572872 | tf_op jit(solution)/shard_map/ppermute | solution.py:12
  28.8 71.5 %copy-start.2 = (bf16[4096,64]{0,1:T(8,128)(2,1)}, bf16[4096,64]{0,1:T(8,128)(2,1)S(1)}, u32[]{:S(2)}) copy-start(bf16[4096,64]{0,1:T(8,128)(2,1)S(1)} %collective-permute-done) | copy-start | bytes 1572868
  30.1 70.2 %collective-permute-start.1 = (bf16[4096,128]{0,1:T(8,128)(2,1)S(1)}, bf16[4096,128]{0,1:T(8,128)(2,1)S(1)}, u32[]{:S(2)}, u32[]{:S(2)}) collective-permute-start(bf16[4096,128]{0,1:T(8,128)(2,1)S(1)} %pad_maximum_fusion.1), channel_id=1, source_target_pairs={{0,24},{4,28},{8,0},{12,4},{16,8},{20,12},{24,16},{28,20},{1,25},{... | collective-permute-start | bytes 3145736 | tf_op jit(solution)/shard_map/ppermute | solution.py:12
  102.9 175.7 %collective-permute-start.2 = (bf16[4096,256]{0,1:T(8,128)(2,1)}, bf16[4096,256]{0,1:T(8,128)(2,1)S(1)}, u32[]{:S(2)}, u32[]{:S(2)}) collective-permute-start(bf16[4096,256]{0,1:T(8,128)(2,1)} %pad_maximum_fusion), channel_id=1, source_target_pairs={{0,16},{4,20},{8,24},{12,28},{16,0},{20,4},{24,8},{28,12},{1,17},{... | collective-permute-start | bytes 6291464 | tf_op jit(solution)/shard_map/ppermute | solution.py:12
  102.9 177.2 %copy-start.1 = (bf16[4096,64]{0,1:T(8,128)(2,1)S(1)}, bf16[4096,64]{0,1:T(8,128)(2,1)}, u32[]{:S(2)}) copy-start(bf16[4096,64]{0,1:T(8,128)(2,1)} %param.8) | copy-start | bytes 1572868
  102.9 178.1 %copy-start.3 = (bf16[4096,64]{0,1:T(8,128)(2,1)S(1)}, bf16[4096,64]{0,1:T(8,128)(2,1)}, u32[]{:S(2)}) copy-start(bf16[4096,64]{0,1:T(8,128)(2,1)} %copy-done.2) | copy-start | bytes 1572868
Sparse Core Ops, SparseCore 0:
  9.5 294.1 all-gather.1
  319.0 28.3 reduce-scatter.1
